TPU v7x, 512 devices: a whole 4x8x8 slice. The times are simulated.
512 devices in a mesh: seq: 64 (over y, z), tp: 8 (over x, core).
Axes of the slice: x: 4, y: 8, z: 8, core: 2. Of those that a mesh axis runs over, the one named last changes fastest.
Arguments:
- queries: bfloat16 [16384, 4096], P('seq', 'tp'), may hold values from -6 to 6
- keys: bfloat16 [16384, 4096], P('seq', 'tp'), may hold values from -6 to 6
- values: bfloat16 [16384, 4096], P('seq', 'tp'), may hold values from -6 to 6
- out_cotangent: bfloat16 [16384, 2048], P('seq', 'tp'), may hold values from -16 to 16
- proj_weight: bfloat16 [4096, 2048], P('tp', 'seq'), may hold values from -0.125 to 0.125
Outputs:
- grad_queries: bfloat16 [16384, 4096], P('seq', 'tp')
- grad_keys: bfloat16 [16384, 4096], P('seq', 'tp')
- grad_values: bfloat16 [16384, 4096], P('seq', 'tp')
- grad_proj: float32 [4096, 2048], P('tp', 'seq')
All inputs are finite; a program needn't handle non-finite values.
Results may differ from a plain program's by a relative error of at most 0.0058.
Values may be sent and summed in bfloat16 or wider, within the bound.
No kernel may reach another device: no remote copies, remote signals or barrier semaphores. Data moves between devices by JAX's collectives and lax.ppermute only.
A program may use at most 128 MiB of HBM per device.

v0:
```python
import jax
import jax.numpy as jnp
from jax import lax
from jax.sharding import PartitionSpec as P

DH = 128


def entering(part, axis, combine, identity, reverse):
    count = lax.axis_size(axis)
    place = lax.axis_index(axis)
    ahead = count - 1 - place if reverse else place
    gathered = lax.all_gather(part, axis)
    state = jnp.zeros_like(part) + jnp.asarray(identity, part.dtype)

    def one(step, state):
        source = count - 1 - step if reverse else step
        return combine(state, lax.dynamic_index_in_dim(gathered, source, 0, False))

    return lax.fori_loop(0, ahead, one, state)


def add_pair(earlier, later_one):
    return earlier + later_one


def per_device(queries, keys, values, out_cotangent, proj_weight):
    tok = queries.shape[0]
    heads = queries.shape[1] // DH
    seq_count = lax.axis_size("seq")
    scale = 1.0 / jnp.sqrt(jnp.float32(DH * tok * seq_count))
    q_heads = queries.reshape(tok, heads, DH)
    k_heads = keys.reshape(tok, heads, DH)
    v_heads = values.reshape(tok, heads, DH)
    kv_state = jnp.einsum("thd,the->hde", k_heads, v_heads, preferred_element_type=jnp.float32)
    zero_state = jnp.zeros_like(kv_state)
    prior_sum = entering(kv_state, "seq", add_pair, zero_state, False)
    full_cot = lax.all_gather(out_cotangent, "tp", axis=1, tiled=True)
    grad_out = lax.dot_general(
        full_cot,
        lax.all_gather(proj_weight, "seq", axis=1, tiled=True),
        (((1,), (1,)), ((), ())),
        preferred_element_type=jnp.float32,
    ).astype(jnp.bfloat16)
    g_heads = grad_out.reshape(tok, heads, DH)
    qg_state = jnp.einsum("thd,the->hde", q_heads, g_heads, preferred_element_type=jnp.float32)
    later_sum = entering(qg_state, "seq", add_pair, zero_state, True)
    prior = prior_sum.astype(jnp.bfloat16)
    later = later_sum.astype(jnp.bfloat16)
    rows = jnp.arange(tok)
    causal = (rows[:, None] >= rows[None, :])[None]
    attn = jnp.where(
        causal,
        jnp.einsum("thd,shd->hts", q_heads, k_heads, preferred_element_type=jnp.float32),
        0.0,
    ).astype(jnp.bfloat16)
    back = jnp.where(
        causal,
        jnp.einsum("thd,shd->hts", g_heads, v_heads, preferred_element_type=jnp.float32),
        0.0,
    ).astype(jnp.bfloat16)
    attn_out = scale * (
        jnp.einsum("hts,she->the", attn, v_heads, preferred_element_type=jnp.float32)
        + jnp.einsum("thd,hde->the", q_heads, prior, preferred_element_type=jnp.float32)
    )
    grad_q = scale * (
        jnp.einsum("hts,shd->thd", back, k_heads, preferred_element_type=jnp.float32)
        + jnp.einsum("the,hde->thd", g_heads, prior, preferred_element_type=jnp.float32)
    )
    grad_k = scale * (
        jnp.einsum("hts,thd->shd", back, q_heads, preferred_element_type=jnp.float32)
        + jnp.einsum("she,hde->shd", v_heads, later, preferred_element_type=jnp.float32)
    )
    grad_v = scale * (
        jnp.einsum("hts,the->she", attn, g_heads, preferred_element_type=jnp.float32)
        + jnp.einsum("shd,hde->she", k_heads, later, preferred_element_type=jnp.float32)
    )
    out_flat = attn_out.astype(jnp.bfloat16).reshape(tok, heads * DH)
    proj_term = lax.dot_general(
        out_flat, full_cot, (((0,), (0,)), ((), ())), preferred_element_type=jnp.float32
    )
    proj_sum = lax.psum_scatter(proj_term, "seq", scatter_dimension=1, tiled=True)
    grad_proj = proj_sum / jnp.sqrt(jnp.float32(tok * seq_count))
    width = heads * DH
    return (
        grad_q.astype(jnp.bfloat16).reshape(tok, width),
        grad_k.astype(jnp.bfloat16).reshape(tok, width),
        grad_v.astype(jnp.bfloat16).reshape(tok, width),
        grad_proj,
    )


def solution(mesh):
    return jax.shard_map(
        per_device,
        mesh=mesh,
        in_specs=(P("seq", "tp"), P("seq", "tp"), P("seq", "tp"), P("seq", "tp"), P("tp", "seq")),
        out_specs=(P("seq", "tp"), P("seq", "tp"), P("seq", "tp"), P("tp", "seq")),
        check_vma=False,
    )
```

profile of v0, /device:TPU:2, one launch (start us, length us, event | category | flops | bytes accessed | tf_op | source)
XLA Modules:
  0.0 670.4 jit_solution(11894771848935743379)
XLA Ops:
  8.7 1.1 copy.56
  9.8 1.9 fusion.17
  11.8 31.1 %all-gather.7.cloned.1.call-done = bf16[256,2048]{1,0:T(8,128)(2,1)} async-done(((bf16[256,256]{1,0:T(8,128)(2,1)}), bf16[256,2048]{1,0:T(8,128)(2,1)}) %all-gather.7.cloned.1.call-update) | async-done | bytes 1048592 | tf_op jit(solution)/shard_map/all_gather | solution.py:38
  42.9 88.4 %all-gather.9.cloned.1.call-done = bf16[512,2048]{0,1:T(8,128)(2,1)} async-done(((bf16[512,32]{0,1:T(8,128)(2,1)}), bf16[512,2048]{0,1:T(8,128)(2,1)}) %all-gather.9.cloned.1.call-update) | async-done | bytes 2097168 | tf_op jit(solution)/shard_map/all_gather | solution.py:41
  131.3 2.6 convolution_convert_fusion
  135.9 135.8 %all-gather.11.cloned.1.call-done = f32[256,128,128]{2,1,0:T(8,128)} async-done(((f32[4,128,128]{2,1,0:T(8,128)}), f32[256,128,128]{2,1,0:T(8,128)}) %all-gather.11.cloned.1.call-update) | async-done | bytes 16777232 | tf_op jit(solution)/shard_map/all_gather | solution.py:13
  272.1 2.7 fusion.35
  277.1 136.3 %all-gather.13.cloned.1.call-done = f32[256,128,128]{2,1,0:T(8,128)} async-done(((f32[4,128,128]{2,1,0:T(8,128)}), f32[256,128,128]{2,1,0:T(8,128)}) %all-gather.13.cloned.1.call-update) | async-done | bytes 16777232 | tf_op jit(solution)/shard_map/all_gather | solution.py:13
  413.4 65.1 %while.23 = (s32[]{:T(128)}, f32[4,128,128]{2,1,0:T(8,128)S(1)}, s32[]{:T(128)}, f32[64,4,128,128]{3,2,1,0:T(8,128)}, s32[]{:T(128)}, /*index=5*/s32[]{:T(128)}, s32[]{:T(128)}, s32[]{:T(128)}) while((s32[]{:T(128)}, f32[4,128,128]{2,1,0:T(8,128)S(1)}, s32[]{:T(128)}, f32[64,4,128,128]{3,2,1,0:T(8,128)}, s32[]{:T(128)}, /*index=5*/s32[]{:T(128)}, ...), condition=%wide.region_3.4_spmd, body=%wide.region_2.3_spmd.sunk | while | flops 65542 | bytes 786575 | solution.py:20
  413.4 1.0 bitcast_add_fusion.5
  414.4 1.0 bitcast_add_fusion.5
  422.7 1.0 bitcast_add_fusion.5
  423.7 1.0 bitcast_add_fusion.5
  424.8 1.0 bitcast_add_fusion.5
  429.9 1.0 bitcast_add_fusion.5
  435.1 1.0 bitcast_add_fusion.5
  436.1 1.0 bitcast_add_fusion.5
  437.2 1.0 bitcast_add_fusion.5
  438.2 1.0 bitcast_add_fusion.5
  439.2 1.0 bitcast_add_fusion.5
  440.3 1.0 bitcast_add_fusion.5
  441.3 1.0 bitcast_add_fusion.5
  443.4 1.0 bitcast_add_fusion.5
  444.4 1.0 bitcast_add_fusion.5
  446.5 1.0 bitcast_add_fusion.5
  447.5 1.0 bitcast_add_fusion.5
  448.5 1.0 bitcast_add_fusion.5
  449.6 1.0 bitcast_add_fusion.5
  450.6 1.0 bitcast_add_fusion.5
  453.7 1.0 bitcast_add_fusion.5
  456.8 1.0 bitcast_add_fusion.5
  457.9 1.0 bitcast_add_fusion.5
  459.9 1.0 bitcast_add_fusion.5
  461.0 1.0 bitcast_add_fusion.5
  462.0 1.0 bitcast_add_fusion.5
  463.0 1.0 bitcast_add_fusion.5
  464.1 1.0 bitcast_add_fusion.5
  465.1 1.0 bitcast_add_fusion.5
  467.2 1.0 bitcast_add_fusion.5
  468.2 1.0 bitcast_add_fusion.5
  470.3 1.0 bitcast_add_fusion.5
  471.3 1.0 bitcast_add_fusion.5
  473.4 1.0 bitcast_add_fusion.5
  474.4 1.0 bitcast_add_fusion.5
  476.5 1.0 bitcast_add_fusion.5
  477.5 1.0 bitcast_add_fusion.5
  480.7 181.7 %reduce-scatter.2.cloned.1.call-done = f32[512,32]{0,1:T(8,128)} async-done(((f32[512,2048]{0,1:T(8,128)}), f32[512,32]{0,1:T(8,128)}) %reduce-scatter.2.cloned.1.call-update) | async-done | bytes 65552 | tf_op jit(solution)/shard_map/reduce_scatter | solution.py:82
  662.4 1.5 broadcast_multiply_fusion
  (62 shorter events, 34.5 us)
Async XLA Ops:
  7.2 126.9 %copy-start = (bf16[256,512]{1,0:T(8,128)(2,1)S(1)}, bf16[256,512]{1,0:T(8,128)(2,1)}, u32[]{:S(2)}) copy-start(bf16[256,512]{1,0:T(8,128)(2,1)} %param.9) | copy-start | bytes 786436
  7.2 128.1 %copy-start.1 = (bf16[256,512]{1,0:T(8,128)(2,1)S(1)}, bf16[256,512]{1,0:T(8,128)(2,1)}, u32[]{:S(2)}) copy-start(bf16[256,512]{1,0:T(8,128)(2,1)} %param.10) | copy-start | bytes 786436
  7.2 35.7 %all-gather.7.cloned.1.call-start = ((), (), s32[]{:S(2)}) async-start(), calls=%async_computation.1 | async-start | bytes 1179648 | tf_op jit(solution)/shard_map/all_gather | solution.py:38
  7.9 123.4 %all-gather.9.cloned.1.call-start = ((), (), s32[]{:S(2)}) async-start(), calls=%async_computation.2 | async-start | bytes 2129920 | tf_op jit(solution)/shard_map/all_gather | solution.py:41
  8.7 263.1 %all-gather.11.cloned.1.call-start = ((), (), s32[]{:S(2)}) async-start(), calls=%async_computation.4 | async-start | bytes 17039360 | tf_op jit(solution)/shard_map/all_gather | solution.py:13
  11.8 401.6 %all-gather.13.cloned.1.call-start = ((), (), s32[]{:S(2)}) async-start(), calls=%async_computation.5 | async-start | bytes 17039360 | tf_op jit(solution)/shard_map/all_gather | solution.py:13
  135.2 527.2 %reduce-scatter.2.cloned.1.call-start = ((), (), s32[]{:S(2)}) async-start(), calls=%async_computation.3 | async-start | bytes 4259840 | tf_op jit(solution)/shard_map/reduce_scatter | solution.py:82
  135.3 136.8 %copy-start.2 = (bf16[256,2048]{1,0:T(8,128)(2,1)S(1)}, bf16[256,2048]{1,0:T(8,128)(2,1)}, u32[]{:S(2)}) copy-start(bf16[256,2048]{1,0:T(8,128)(2,1)} %all-gather.7.cloned.1.call-done) | copy-start | bytes 3145732
Sparse Core Ops, SparseCore 0:
  10.1 32.7 all-gather.6
  45.9 85.3 all-gather.8
  134.9 136.7 all-gather.10
  275.2 138.1 all-gather.12
  417.3 245.0 reduce-scatter.1
where the time goes:
time: 673 us; the launch traced here: 670 us
  waiting for transfers between devices  575 us (85%)
  other arithmetic  65.2 us (10%)
  between operations  13.9 us (2%)
  matrix products  10.2 us (2%)
    all_gather x2, waiting for transfers between devices, entering(): gathered = lax.all_gather(part, axis)  272 us
    reduce_scatter x1, waiting for transfers between devices, per_device(): lax.psum_scatter(proj_term, 'seq', scatter_dimension=1, tiled=True)  182 us
    all_gather x1, waiting for transfers between devices, per_device(): lax.all_gather(proj_weight, 'seq', axis=1, tiled=True)  88.4 us
    add x63, other arithmetic, add_pair(): return earlier + later_one  63.7 us
    all_gather x1, waiting for transfers between devices, per_device(): full_cot = lax.all_gather(out_cotangent, 'tp', axis=1, tiled=True)  31.1 us
  transfers between devices with their start and end apart: 5, of which 5 were waited for; matrix products, arithmetic and copies ran while one was open for 12% of the time, Pallas kernels for 0%

commit v1 on v0

--- a/solution.py
+++ b/solution.py
@@ -1,9 +1,34 @@
+import functools
 import jax
 import jax.numpy as jnp
 from jax import lax
 from jax.sharding import PartitionSpec as P
 
 DH = 128
+
+
+def bind_the_cubes(vals, peer_axis):
+    reached = lax.axis_size(peer_axis)
+    aux, moved, carry_out = (reached, lax.axis_index(peer_axis), vals.shape[1])
+    sides = list(map(lambda q: (q, (q + 1) % aux), range(aux)))
+    carry = map(lambda q: (q, (q - 1) % aux), range(aux))
+    nodes = list(carry)
+    h_now = jnp.zeros((*vals.shape[:1], aux * carry_out, *vals.shape[2:]), vals.dtype)
+    h_now = lax.dynamic_update_slice_in_dim(h_now, vals, moved * carry_out, axis=1)
+    mixed_arr = aux // 2
+    z_new = t_next = vals
+    for h in range(1, mixed_arr + 1):
+        z_new = lax.ppermute(z_new, peer_axis, sides)
+        h_now = lax.dynamic_update_slice_in_dim(h_now, z_new, (moved - h) % aux * carry_out, axis=1)
+        if h < aux - mixed_arr:
+            t_next = lax.ppermute(t_next, peer_axis, nodes)
+            h_now = lax.dynamic_update_slice_in_dim(
+                h_now, t_next, (moved + h) % aux * carry_out, axis=1
+            )
+    return h_now
+
+
+tiles_show = functools.partial(bind_the_cubes, peer_axis="tp")
 
 
 def entering(part, axis, combine, identity, reverse):
@@ -35,7 +60,7 @@
     kv_state = jnp.einsum("thd,the->hde", k_heads, v_heads, preferred_element_type=jnp.float32)
     zero_state = jnp.zeros_like(kv_state)
     prior_sum = entering(kv_state, "seq", add_pair, zero_state, False)
-    full_cot = lax.all_gather(out_cotangent, "tp", axis=1, tiled=True)
+    full_cot = tiles_show(out_cotangent)
     grad_out = lax.dot_general(
         full_cot,
         lax.all_gather(proj_weight, "seq", axis=1, tiled=True),

time: 673 us -> 641 us (0.952)
  waiting for transfers between devices: 575 us -> 535 us
  starting transfers between devices: 0.2 us -> 7.56 us
    all_gather x1 -> x0, waiting for transfers between devices: 31.1 us -> none  [per_device(): full_cot = lax.all_gather(out_cotangent, 'tp', axis=1, tiled=True)]
    all_gather x1, waiting for transfers between devices: 88.4 us -> 67.4 us  [per_device(): lax.all_gather(proj_weight, 'seq', axis=1, tiled=True)]
    ppermute x0 -> x7, waiting for transfers between devices: none -> 12.3 us  [the longest x4 12.3 us: bind_the_cubes(): z_new = lax.ppermute(z_new, peer_axis, sides)]
    ppermute x0 -> x7, starting transfers between devices: none -> 7.4 us  [the longest x3 7.37 us: bind_the_cubes(): t_next = lax.ppermute(t_next, peer_axis, nodes)]
  transfers between devices with their start and end apart: 5 -> 11, of which waited for: 5 -> 8; matrix products, arithmetic and copies ran while one was open for 12% -> 12% of each run, Pallas kernels for 0% -> 0%
where the time goes in v1:
time: 641 us; the launch traced here: 639 us
  waiting for transfers between devices  535 us (83%)
  other arithmetic  65.2 us (10%)
  between operations  14 us (2%)
  matrix products  9.87 us (2%)
  starting transfers between devices  7.56 us (1%)
    all_gather x2, waiting for transfers between devices, entering(): gathered = lax.all_gather(part, axis)  273 us
    reduce_scatter x1, waiting for transfers between devices, per_device(): lax.psum_scatter(proj_term, 'seq', scatter_dimension=1, tiled=True)  181 us
    all_gather x1, waiting for transfers between devices, per_device(): lax.all_gather(proj_weight, 'seq', axis=1, tiled=True)  67.4 us
    add x63, other arithmetic, add_pair(): return earlier + later_one  63.7 us
  transfers between devices with their start and end apart: 11, of which 8 were waited for; matrix products, arithmetic and copies ran while one was open for 12% of the time, Pallas kernels for 0%

profile of v1, /device:TPU:2, one launch (start us, length us, event | category | flops | bytes accessed | tf_op | source)
XLA Modules:
  0.0 638.7 jit_solution(18164911491396075937)
XLA Ops:
  8.0 1.1 copy.56
  9.1 1.9 fusion.17
  11.1 1.7 collective-permute-start.1
  13.9 1.8 collective-permute-done
  15.7 2.6 collective-permute-start.3
  18.4 2.5 collective-permute-done.2
  20.9 3.0 collective-permute-start.5
  23.9 2.5 collective-permute-done.4
  26.5 5.5 collective-permute-done.6
  32.0 67.4 %all-gather.6.cloned.1.call-done = bf16[512,2048]{0,1:T(8,128)(2,1)} async-done(((bf16[512,32]{0,1:T(8,128)(2,1)}), bf16[512,2048]{0,1:T(8,128)(2,1)}) %all-gather.6.cloned.1.call-update) | async-done | bytes 2097168 | tf_op jit(solution)/shard_map/all_gather | solution.py:66
  99.5 2.3 convolution_convert_fusion
  103.7 136.2 %all-gather.8.cloned.1.call-done = f32[256,128,128]{2,1,0:T(8,128)} async-done(((f32[4,128,128]{2,1,0:T(8,128)}), f32[256,128,128]{2,1,0:T(8,128)}) %all-gather.8.cloned.1.call-update) | async-done | bytes 16777232 | tf_op jit(solution)/shard_map/all_gather | solution.py:38
  240.2 2.7 fusion.35
  245.1 136.5 %all-gather.10.cloned.1.call-done = f32[256,128,128]{2,1,0:T(8,128)} async-done(((f32[4,128,128]{2,1,0:T(8,128)}), f32[256,128,128]{2,1,0:T(8,128)}) %all-gather.10.cloned.1.call-update) | async-done | bytes 16777232 | tf_op jit(solution)/shard_map/all_gather | solution.py:38
  381.6 65.4 %while.23 = (s32[]{:T(128)}, f32[4,128,128]{2,1,0:T(8,128)S(1)}, s32[]{:T(128)}, f32[64,4,128,128]{3,2,1,0:T(8,128)}, s32[]{:T(128)}, /*index=5*/s32[]{:T(128)}, s32[]{:T(128)}, s32[]{:T(128)}) while((s32[]{:T(128)}, f32[4,128,128]{2,1,0:T(8,128)S(1)}, s32[]{:T(128)}, f32[64,4,128,128]{3,2,1,0:T(8,128)}, s32[]{:T(128)}, /*index=5*/s32[]{:T(128)}, ...), condition=%wide.region_3.4_spmd, body=%wide.region_2.3_spmd.sunk | while | flops 65542 | bytes 786567 | solution.py:45
  382.7 1.0 bitcast_add_fusion.5
  386.8 1.0 bitcast_add_fusion.5
  391.0 1.0 bitcast_add_fusion.5
  394.1 1.0 bitcast_add_fusion.5
  398.3 1.0 bitcast_add_fusion.5
  403.4 1.0 bitcast_add_fusion.5
  404.5 1.0 bitcast_add_fusion.5
  408.6 1.0 bitcast_add_fusion.5
  409.7 1.0 bitcast_add_fusion.5
  411.8 1.0 bitcast_add_fusion.5
  412.8 1.0 bitcast_add_fusion.5
  414.9 1.0 bitcast_add_fusion.5
  415.9 1.0 bitcast_add_fusion.5
  418.0 1.0 bitcast_add_fusion.5
  419.0 1.0 bitcast_add_fusion.5
  422.1 1.0 bitcast_add_fusion.5
  424.2 1.0 bitcast_add_fusion.5
  425.3 1.0 bitcast_add_fusion.5
  426.3 1.0 bitcast_add_fusion.5
  428.4 1.0 bitcast_add_fusion.5
  429.4 1.0 bitcast_add_fusion.5
  431.5 1.0 bitcast_add_fusion.5
  432.5 1.0 bitcast_add_fusion.5
  435.7 1.0 bitcast_add_fusion.5
  436.7 1.0 bitcast_add_fusion.5
  438.8 1.0 bitcast_add_fusion.5
  439.8 1.0 bitcast_add_fusion.5
  441.9 1.0 bitcast_add_fusion.5
  442.9 1.0 bitcast_add_fusion.5
  445.0 1.0 bitcast_add_fusion.5
  446.0 1.0 bitcast_add_fusion.5
  449.3 181.5 %reduce-scatter.2.cloned.1.call-done = f32[512,32]{0,1:T(8,128)} async-done(((f32[512,2048]{0,1:T(8,128)}), f32[512,32]{0,1:T(8,128)}) %reduce-scatter.2.cloned.1.call-update) | async-done | bytes 65552 | tf_op jit(solution)/shard_map/reduce_scatter | solution.py:107
  630.7 1.5 broadcast_multiply_fusion
  (80 shorter events, 41.0 us)
Async XLA Ops:
  7.2 94.7 %copy-start = (bf16[256,512]{1,0:T(8,128)(2,1)S(1)}, bf16[256,512]{1,0:T(8,128)(2,1)}, u32[]{:S(2)}) copy-start(bf16[256,512]{1,0:T(8,128)(2,1)} %param.9) | copy-start | bytes 786436
  7.2 92.3 %all-gather.6.cloned.1.call-start = ((), (), s32[]{:S(2)}) async-start(), calls=%async_computation.1 | async-start | bytes 2129920 | tf_op jit(solution)/shard_map/all_gather | solution.py:66
  7.9 231.9 %all-gather.8.cloned.1.call-start = ((), (), s32[]{:S(2)}) async-start(), calls=%async_computation.3 | async-start | bytes 17039360 | tf_op jit(solution)/shard_map/all_gather | solution.py:38
  11.0 370.6 %all-gather.10.cloned.1.call-start = ((), (), s32[]{:S(2)}) async-start(), calls=%async_computation.4 | async-start | bytes 17039360 | tf_op jit(solution)/shard_map/all_gather | solution.py:38
  11.1 4.6 collective-permute-start
  11.1 4.6 collective-permute-start.1
  12.9 90.1 %copy-start.1 = (bf16[256,512]{1,0:T(8,128)(2,1)S(1)}, bf16[256,512]{1,0:T(8,128)(2,1)}, u32[]{:S(2)}) copy-start(bf16[256,512]{1,0:T(8,128)(2,1)} %param.10) | copy-start | bytes 786436
  15.7 5.2 collective-permute-start.2
  15.7 5.2 collective-permute-start.3
  20.9 5.5 collective-permute-start.4
  20.9 5.5 collective-permute-start.5
  26.4 5.6 collective-permute-start.6
  103.0 527.8 %reduce-scatter.2.cloned.1.call-start = ((), (), s32[]{:S(2)}) async-start(), calls=%async_computation.2 | async-start | bytes 4259840 | tf_op jit(solution)/shard_map/reduce_scatter | solution.py:107
Sparse Core Ops, SparseCore 0:
  11.0 88.3 all-gather.5
  103.0 136.7 all-gather.7
  243.4 138.1 all-gather.9
  385.5 245.1 reduce-scatter.1
